TPU v7x, 32 devices: a whole 2x2x4 slice. The times are simulated.
32 devices in a mesh: dp: 16 (over z, y, x), mp: 2 (over core).
Axes of the slice: x: 2, y: 2, z: 4, core: 2. Of those that a mesh axis runs over, the one named last changes fastest.
Arguments:
- gradients: float32 [16, 4, 32, 8192], P('dp', None, 'mp'), may hold values from -6 to 6
- weights: float32 [4, 32, 8192], P(None, 'mp', 'dp'), may hold values from -40 to 40
- first_moment: float32 [4, 32, 8192], P(None, 'mp', 'dp'), may hold values from -0.6 to 0.6
- second_moment: float32 [4, 32, 8192], P(None, 'mp', 'dp'), may hold values from 0.001 to 0.1
- learn_rate: float32 [4], replicated, may hold values from 0.1 to 0.5
- weight_decay: float32 [4], replicated, may hold values from 0.1 to 1
Outputs:
- new_weights: float32 [4, 32, 8192], P(None, 'mp')
- new_first: float32 [4, 32, 8192], P(None, 'mp', 'dp')
- new_second: float32 [4, 32, 8192], P(None, 'mp', 'dp')
- trust_ratio: float32 [4], replicated
All inputs are finite; a program needn't handle non-finite values.
Results may differ from a plain program's by a relative error of at most 0.000062.
Values sent between devices are 32-bit elements; how exact they have to be, the bound alone decides.
No kernel may reach another device: no remote copies, remote signals or barrier semaphores. Data moves between devices by JAX's collectives and lax.ppermute only.
A program may use at most 64 MiB of HBM per device.

v0:
```python
import jax
import jax.numpy as jnp
from jax import lax
from jax.sharding import PartitionSpec as P

STEP = 10


def shards(gradients, weights, first_moment, second_moment, learn_rate, weight_decay):
    replicas = lax.axis_size("dp")
    summed = lax.psum_scatter(gradients, "dp", scatter_dimension=3, tiled=True)[0] * (
        1.0 / replicas
    )
    new_first = 0.9 * first_moment + 0.1 * summed
    new_second = 0.999 * second_moment + 0.001 * summed * summed
    first_fix = 1.0 - 0.9**STEP
    second_fix = 1.0 - 0.999**STEP
    update = (
        new_first / first_fix / (jnp.sqrt(new_second / second_fix) + 1e-06)
        + weight_decay[:, None, None] * weights
    )
    weight_sq, update_sq = lax.psum(
        (jnp.sum(weights * weights, axis=(1, 2)), jnp.sum(update * update, axis=(1, 2))),
        ("dp", "mp"),
    )
    trust_ratio = jnp.sqrt(weight_sq) / (jnp.sqrt(update_sq) + 1e-06)
    stepped = weights - (learn_rate * trust_ratio)[:, None, None] * update
    new_weights = lax.all_gather(stepped, "dp", axis=2, tiled=True)
    return (new_weights, new_first, new_second, trust_ratio)


def solution(mesh):
    in_specs = (
        P("dp", None, "mp", None),
        P(None, "mp", "dp"),
        P(None, "mp", "dp"),
        P(None, "mp", "dp"),
        P(),
        P(),
    )
    out_specs = (P(None, "mp", None), P(None, "mp", "dp"), P(None, "mp", "dp"), P())
    return jax.shard_map(shards, mesh=mesh, in_specs=in_specs, out_specs=out_specs, check_vma=False)
```

profile of v0, /device:TPU:0, one launch (start us, length us, event | category | flops | bytes accessed | tf_op | source)
XLA Modules:
  0.0 205.5 jit_solution(638651230014546051)
XLA Ops:
  7.2 0.0 copy-start
  7.2 0.0 copy-start.3
  7.2 0.0 copy-start.2
  7.2 0.0 copy-start.1
  7.2 0.0 copy-start.4
  7.2 0.0 reduce-scatter.2.cloned.1.call-start
  7.3 0.7 reduce-scatter.2.cloned.1.call-update
  7.9 0.0 all-gather.2.cloned.1.call-start
  8.0 86.7 %reduce-scatter.2.cloned.1.call-done = f32[1,4,16,512]{3,2,1,0:T(8,128)} async-done(((f32[1,4,16,8192]{3,2,1,0:T(8,128)}), f32[1,4,16,512]{3,2,1,0:T(8,128)}) %reduce-scatter.2.cloned.1.call-update) | async-done | bytes 131088 | tf_op jit(solution)/shard_map/reduce_scatter | solution.py:11
  94.7 0.0 copy-done
  94.7 0.0 copy-done.3
  94.7 0.0 copy-done.2
  94.7 0.0 copy-done.1
  94.7 1.7 multiply_reduce_fusion
  96.4 36.8 %all-reduce = (f32[4]{0:T(128)S(1)}, f32[4]{0:T(128)S(1)}) all-reduce(f32[4]{0:T(128)S(1)} %get-tuple-element.8, f32[4]{0:T(128)S(1)} %get-tuple-element.12), channel_id=1, replica_groups=mesh['dp'=16,'mp'=2] {'dp','mp'}, use_global_device_ids=true, to_apply=%region_4.0 | all-reduce | flops 8 | bytes 64 | tf_op jit(solution)/shard_map/psum | solution.py:22
  133.2 0.0 copy-done.4
  133.2 0.5 fusion
  133.7 0.7 multiply_subtract_fusion
  134.4 0.0 all-gather.2.cloned.1.call-update
  134.5 61.1 %all-gather.2.cloned.1.call-done = f32[4,16,8192]{2,1,0:T(8,128)} async-done(((f32[4,16,512]{2,1,0:T(8,128)}), f32[4,16,8192]{2,1,0:T(8,128)}) %all-gather.2.cloned.1.call-update) | async-done | bytes 2097168 | tf_op jit(solution)/shard_map/all_gather | solution.py:28
  195.6 3.1 %copy.11 = f32[4,16,8192]{2,1,0:T(8,128)} copy(f32[4,16,8192]{2,1,0:T(8,128)} %all-gather.2.cloned.1.call-done) | data formatting | bytes 4194304
Async XLA Ops:
  7.2 87.5 %copy-start = (f32[4,16,512]{2,1,0:T(8,128)S(1)}, f32[4,16,512]{2,1,0:T(8,128)}, u32[]{:S(2)}) copy-start(f32[4,16,512]{2,1,0:T(8,128)} %param.7) | copy-start | bytes 393220
  7.2 87.5 %copy-start.3 = (f32[4]{0:T(128)S(1)}, f32[4]{0:T(128)}, u32[]{:S(2)}) copy-start(f32[4]{0:T(128)} %param.11) | copy-start | bytes 52
  7.2 87.5 %copy-start.2 = (f32[4,16,512]{2,1,0:T(8,128)S(1)}, f32[4,16,512]{2,1,0:T(8,128)}, u32[]{:S(2)}) copy-start(f32[4,16,512]{2,1,0:T(8,128)} %param.9) | copy-start | bytes 393220
  7.2 87.5 %copy-start.1 = (f32[4,16,512]{2,1,0:T(8,128)S(1)}, f32[4,16,512]{2,1,0:T(8,128)}, u32[]{:S(2)}) copy-start(f32[4,16,512]{2,1,0:T(8,128)} %param.8) | copy-start | bytes 393220
  7.2 126.0 %copy-start.4 = (f32[4]{0:T(128)S(1)}, f32[4]{0:T(128)}, u32[]{:S(2)}) copy-start(f32[4]{0:T(128)} %param.10) | copy-start | bytes 52
  7.2 87.4 %reduce-scatter.2.cloned.1.call-start = ((), (), s32[]{:S(2)}) async-start(), calls=%async_computation.1 | async-start | bytes 2228224 | tf_op jit(solution)/shard_map/reduce_scatter | solution.py:11
  7.9 187.6 %all-gather.2.cloned.1.call-start = ((), (), s32[]{:S(2)}) async-start(), calls=%async_computation.2 | async-start | bytes 2228224 | tf_op jit(solution)/shard_map/all_gather | solution.py:28
Sparse Core Ops, SparseCore 0:
  10.3 84.3 reduce-scatter.1
  134.6 60.9 all-gather.1
where the time goes:
time: 206 us; the launch traced here: 205 us
  waiting for transfers between devices  148 us (72%)
  blocking collectives  36.8 us (18%)
  between operations  14.1 us (7%)
  local copies, waits for them, and re-layouts  3.08 us (1%)
  other arithmetic  2.97 us (1%)
    reduce_scatter x1, waiting for transfers between devices, shards(): lax.psum_scatter(gradients, 'dp', scatter_dimension=3, tiled=True)[0]  86.7 us
    all_gather x1, waiting for transfers between devices, shards(): new_weights = lax.all_gather(stepped, 'dp', axis=2, tiled=True)  61.1 us
    psum x1, blocking collectives, shards(): lax.psum((jnp.sum(weights * weights, axis=(1, 2)), jnp.sum(update * updat...  36.8 us
  transfers between devices with their start and end apart: 2, of which 2 were waited for; matrix products, arithmetic and copies ran while one was open for 0% of the time, Pallas kernels for 0%

commit v1 on v0

v1 whole, which is shorter than its diff:
```python
import jax
import jax.numpy as jnp
from jax import lax
from jax.sharding import PartitionSpec as P

STEP = 10
SUB, LANE = 8, 128


def tiles(a):
    t, r, c = a.shape
    a = a.reshape(t, r // SUB, SUB, c // LANE, LANE)
    return a.transpose(0, 1, 3, 2, 4).reshape(t * (r // SUB), c // LANE, SUB, LANE)


def untiles(a, t, r):
    c = a.shape[1]
    a = a.reshape(t, r // SUB, c, SUB, LANE).transpose(0, 1, 3, 2, 4)
    return a.reshape(t, r, c * LANE)


def swap(a, axis, bit):
    n = lax.axis_size(axis)
    return lax.ppermute(a, axis, [(i, i ^ (1 << bit)) for i in range(n)])


def pick(a, k):
    return lax.dynamic_index_in_dim(a, k, 1, keepdims=False)


class Block:
    def __init__(self, addends, left):
        self.addends, self.left = addends, left

    def halves(self, bit, b):
        at = self.left.index(bit)
        send, keep = [], []
        for a in self.addends:
            send.append(lax.dynamic_index_in_dim(a, 1 - b, 1 + at, keepdims=False))
            keep.append(lax.dynamic_index_in_dim(a, b, 1 + at, keepdims=False))
        left = tuple(x for x in self.left if x != bit)
        return sum(send[1:], send[0]), Block(keep, left)


def shards(gradients, weights, first_moment, second_moment, learn_rate, weight_decay):
    n = lax.axis_size("dp")
    bits = n.bit_length() - 1
    me = lax.axis_index("dp")
    b = [(me >> i) & 1 for i in range(bits)]
    nt, rows, _ = weights.shape
    g = tiles(gradients[0])
    high = tuple(reversed(range(bits)))
    g = g.reshape((g.shape[0],) + (2,) * bits + (g.shape[1] // n, SUB, LANE))
    half = g.shape[0] // 2
    pair = [Block([g[:half]], high), Block([g[half:]], high)]
    orders = [(0, 1), (1, 0)]
    for phase in range(2):
        for s in range(2):
            bit = orders[s][phase]
            send, pair[s] = pair[s].halves(bit, b[bit])
            pair[s].addends.append(swap(send, "dp", bit))
    whole = Block([jnp.concatenate([sum(p.addends[1:], p.addends[0]) for p in pair])], pair[0].left)
    for bit in range(2, bits):
        send, whole = whole.halves(bit, b[bit])
        whole.addends.append(swap(send, "dp", bit))
    summed = sum(whole.addends[1:], whole.addends[0]) * (1.0 / n)

    w, m, v = tiles(weights), tiles(first_moment), tiles(second_moment)
    per = w.shape[0] // nt
    new_first = 0.9 * m + 0.1 * summed
    new_second = 0.999 * v + 0.001 * summed * summed
    first_fix = 1.0 - 0.9**STEP
    second_fix = 1.0 - 0.999**STEP
    decay = jnp.repeat(weight_decay, per)[:, None, None, None]
    update = new_first / first_fix / (jnp.sqrt(new_second / second_fix) + 1e-06) + decay * w

    def squares(a):
        return jnp.sum((a * a).reshape(nt, -1), axis=1)

    sq = jnp.stack([squares(w), squares(update)])
    for axis in ("mp", "dp"):
        for bit in range(lax.axis_size(axis).bit_length() - 1):
            sq = sq + swap(sq, axis, bit)
    trust_ratio = jnp.sqrt(sq[0]) / (jnp.sqrt(sq[1]) + 1e-06)
    rate = jnp.repeat(learn_rate * trust_ratio, per)[:, None, None, None]
    full = w - rate * update

    def joined(a, bit, at):
        other = swap(a, "dp", bit)
        low, high = jnp.where(b[bit] == 0, a, other), jnp.where(b[bit] == 0, other, a)
        return jnp.stack([low, high], axis=at)

    for bit in reversed(range(2, bits)):
        full = joined(full, bit, 1 + bits - 1 - bit)
    pair = [full[:half], full[half:]]
    for phase in reversed(range(2)):
        pair = [joined(pair[s], orders[s][phase], bits - 1 + (1 - phase if s == 0 else 0)) for s in range(2)]
    full = jnp.concatenate(pair)
    full = full.reshape(full.shape[0], -1, SUB, LANE)
    return (
        untiles(full, nt, rows),
        untiles(new_first, nt, rows),
        untiles(new_second, nt, rows),
        trust_ratio,
    )


def solution(mesh):
    in_specs = (
        P("dp", None, "mp", None),
        P(None, "mp", "dp"),
        P(None, "mp", "dp"),
        P(None, "mp", "dp"),
        P(),
        P(),
    )
    out_specs = (P(None, "mp", None), P(None, "mp", "dp"), P(None, "mp", "dp"), P())
    return jax.shard_map(shards, mesh=mesh, in_specs=in_specs, out_specs=out_specs, check_vma=False)
```

time: 206 us -> 98.8 us (0.48)
  waiting for transfers between devices: 148 us -> 63 us
  blocking collectives: 36.8 us -> 0 us
  starting transfers between devices: 0.08 us -> 22.5 us
  between operations: 14.1 us -> 0.84 us
  other arithmetic: 2.97 us -> 8.41 us
    reduce_scatter x1 -> x0, waiting for transfers between devices: 86.7 us -> none  [shards(): lax.psum_scatter(gradients, 'dp', scatter_dimension=3, tiled=True)[0]]
    ppermute x0 -> x17, waiting for transfers between devices: none -> 63 us  [swap(): return lax.ppermute(a, axis, [(i, i ^ 1 << bit) for i in range(n)])]
    all_gather x1 -> x0, waiting for transfers between devices: 61.1 us -> none  [shards(): new_weights = lax.all_gather(stepped, 'dp', axis=2, tiled=True)]
    psum x1 -> x0, blocking collectives: 36.8 us -> none  [shards(): lax.psum((jnp.sum(weights * weights, axis=(1, 2)), jnp.sum(update * updat...]
    ppermute x0 -> x17, starting transfers between devices: none -> 22.5 us  [swap(): return lax.ppermute(a, axis, [(i, i ^ 1 << bit) for i in range(n)])]
    unnamed x11 -> x6, local copies, waits for them, and re-layouts: 3.08 us -> 0.01 us
    add x0 -> x10, other arithmetic: none -> 2.83 us  [the longest x2 2.01 us: shards(): sum(p.addends[1:], p.addends[0])]
  transfers between devices with their start and end apart: 2 -> 17, of which waited for: 2 -> 16; matrix products, arithmetic and copies ran while one was open for 0% -> 5% of each run, Pallas kernels for 0% -> 0%
where the time goes in v1:
time: 98.8 us; the launch traced here: 98.6 us
  waiting for transfers between devices  63 us (64%)
  starting transfers between devices  22.5 us (23%)
  other arithmetic  8.41 us (9%)
  local copies, waits for them, and re-layouts  3.8 us (4%)
    ppermute x17, waiting for transfers between devices, swap(): return lax.ppermute(a, axis, [(i, i ^ 1 << bit) for i in range(n)])  63 us
    ppermute x17, starting transfers between devices, swap(): return lax.ppermute(a, axis, [(i, i ^ 1 << bit) for i in range(n)])  22.5 us
    add x2, other arithmetic, shards(): sum(p.addends[1:], p.addends[0])  2.01 us
  transfers between devices with their start and end apart: 17, of which 16 were waited for; matrix products, arithmetic and copies ran while one was open for 5% of the time, Pallas kernels for 0%

profile of v1, /device:TPU:0, one launch (start us, length us, event | category | flops | bytes accessed | tf_op | source)
XLA Modules:
  0.0 98.6 jit_solution(17193573508172239452)
XLA Ops:
  0.6 1.7 %fusion.17 = (f32[2,2,64,8,128]{4,3,2,1,0:T(8,128)S(1)}, f32[2,2,64,8,128]{4,3,2,1,0:T(8,128)S(1)}) fusion(f32[4,2,64,8,128]{4,3,2,1,0:T(8,128)} %bitcast.121), kind=kLoop, calls=%fused_computation.58 | loop fusion | bytes 4194304 | tf_op jit(solution)/shard_map/slice | solution.py:55
  2.3 0.9 dynamic-slice_bitcast_fusion
  3.2 3.0 %collective-permute-start.2 = (f32[4,2,2,2,4,8,128]{6,5,4,3,2,1,0:T(8,128)}, f32[4,2,2,2,4,8,128]{6,5,4,3,2,1,0:T(8,128)S(1)}, u32[]{:S(2)}, u32[]{:S(2)}) collective-permute-start(f32[4,2,2,2,4,8,128]{6,5,4,3,2,1,0:T(8,128)} %dynamic-slice_bitcast_fusion), channel_id=1, source_target_pairs={{0,4},{2,6},{4,0},{6,2},{8,12},{10,14},{12,8},{14,10},{16,20},{18,... | collective-permute-start | bytes 1572872 | tf_op jit(solution)/shard_map/ppermute | solution.py:24
  6.2 0.8 dynamic-slice_bitcast_fusion.1
  7.0 1.5 %collective-permute-start = (f32[4,2,2,2,4,8,128]{6,5,4,3,2,1,0:T(8,128)}, f32[4,2,2,2,4,8,128]{6,5,4,3,2,1,0:T(8,128)S(1)}, u32[]{:S(2)}, u32[]{:S(2)}) collective-permute-start(f32[4,2,2,2,4,8,128]{6,5,4,3,2,1,0:T(8,128)} %dynamic-slice_bitcast_fusion.1), channel_id=1, source_target_pairs={{0,2},{2,0},{4,6},{6,4},{8,10},{10,8},{12,14},{14,12},{16,18},{18,... | collective-permute-start | bytes 1572872 | tf_op jit(solution)/shard_map/ppermute | solution.py:24
  8.5 9.8 %collective-permute-done.2 = f32[4,2,2,2,4,8,128]{6,5,4,3,2,1,0:T(8,128)S(1)} collective-permute-done((f32[4,2,2,2,4,8,128]{6,5,4,3,2,1,0:T(8,128)}, f32[4,2,2,2,4,8,128]{6,5,4,3,2,1,0:T(8,128)S(1)}, u32[]{:S(2)}, u32[]{:S(2)}) %collective-permute-start.2) | collective-permute-done | bytes 524320 | tf_op jit(solution)/shard_map/ppermute | solution.py:24
  18.4 1.8 %collective-permute-start.3 = (f32[4,2,2,4,8,128]{5,4,3,2,1,0:T(8,128)S(1)}, f32[4,2,2,4,8,128]{5,4,3,2,1,0:T(8,128)}, u32[]{:S(2)}, u32[]{:S(2)}) collective-permute-start(f32[4,2,2,4,8,128]{5,4,3,2,1,0:T(8,128)S(1)} %bitcast_add_fusion), channel_id=1, source_target_pairs={{0,2},{2,0},{4,6},{6,4},{8,10},{10,8},{12,14},{14,12},{16,18},{18,... | collective-permute-start | bytes 786440 | tf_op jit(solution)/shard_map/ppermute | solution.py:24
  20.1 0.8 collective-permute-done
  21.0 0.7 bitcast_add_fusion.2
  21.7 0.7 collective-permute-start.1
  22.4 3.9 %collective-permute-done.3 = f32[4,2,2,4,8,128]{5,4,3,2,1,0:T(8,128)} collective-permute-done((f32[4,2,2,4,8,128]{5,4,3,2,1,0:T(8,128)S(1)}, f32[4,2,2,4,8,128]{5,4,3,2,1,0:T(8,128)}, u32[]{:S(2)}, u32[]{:S(2)}) %collective-permute-start.3) | collective-permute-done | bytes 262176 | tf_op jit(solution)/shard_map/ppermute | solution.py:24
  26.3 1.0 %fusion.3 = f32[4,2,2,4,8,128]{5,4,3,2,1,0:T(8,128)S(1)} fusion(f32[4,2,2,4,8,128]{5,4,3,2,1,0:T(8,128)} %collective-permute-done.3, f32[4,2,2,2,4,8,128]{6,5,4,3,2,1,0:T(8,128)S(1)} %collective-permute-done.2, s32[]{:T(128)S(6)} %select_n.127, f32[4,2,2,2,2,4,8,128]{7,6,5,4,3,2,1,0:T(8,128)S(1)} %bitcast.120, s32[]{:T(128)S(6)} %select_n.126, s32[]{:T(128)S(6)} %select_n.128), kind=kLoop, calls=%fused_computation.25 | loop fusion | flops 131072 | bytes 1048588 | tf_op jit(solution)/shard_map/add | solution.py:62
  27.4 1.2 %collective-permute-done.1 = f32[4,2,2,4,8,128]{5,4,3,2,1,0:T(8,128)} collective-permute-done((f32[4,2,2,4,8,128]{5,4,3,2,1,0:T(8,128)}, f32[4,2,2,4,8,128]{5,4,3,2,1,0:T(8,128)}, u32[]{:S(2)}, u32[]{:S(2)}) %collective-permute-start.1) | collective-permute-done | bytes 262176 | tf_op jit(solution)/shard_map/ppermute | solution.py:24
  28.6 1.0 %fusion.4 = f32[4,2,2,4,8,128]{5,4,3,2,1,0:T(8,128)S(1)} fusion(f32[4,2,2,4,8,128]{5,4,3,2,1,0:T(8,128)} %collective-permute-done.1, f32[4,2,2,2,4,8,128]{6,5,4,3,2,1,0:T(8,128)S(1)} %collective-permute-done, s32[]{:T(128)S(6)} %select_n.125, f32[4,2,2,2,2,4,8,128]{7,6,5,4,3,2,1,0:T(8,128)S(1)} %bitcast.117, s32[]{:T(128)S(6)} %select_n.126, s32[]{:T(128)S(6)} %select_n.128), kind=kLoop, calls=%fused_computation.28 | loop fusion | flops 131072 | bytes 1048588 | tf_op jit(solution)/shard_map/add | solution.py:62
  29.6 1.6 %collective-permute-start.4 = (f32[8,2,4,8,128]{4,3,2,1,0:T(8,128)S(1)}, f32[8,2,4,8,128]{4,3,2,1,0:T(8,128)S(1)}, u32[]{:S(2)}, u32[]{:S(2)}) collective-permute-start(f32[8,2,4,8,128]{4,3,2,1,0:T(8,128)S(1)} %fusion.2), channel_id=1, source_target_pairs={{0,8},{2,10},{4,12},{6,14},{8,0},{10,2},{12,4},{14,6},{16,24},{18,... | collective-permute-start | bytes 786440 | tf_op jit(solution)/shard_map/ppermute | solution.py:24
  31.3 0.9 broadcast_multiply_fusion.1
  32.2 3.9 %collective-permute-done.4 = f32[8,2,4,8,128]{4,3,2,1,0:T(8,128)S(1)} collective-permute-done((f32[8,2,4,8,128]{4,3,2,1,0:T(8,128)S(1)}, f32[8,2,4,8,128]{4,3,2,1,0:T(8,128)S(1)}, u32[]{:S(2)}, u32[]{:S(2)}) %collective-permute-start.4) | collective-permute-done | bytes 262176 | tf_op jit(solution)/shard_map/ppermute | solution.py:24
  36.1 3.8 %collective-permute-start.5 = (f32[8,4,8,128]{3,2,1,0:T(8,128)S(1)}, f32[8,4,8,128]{3,2,1,0:T(8,128)S(1)}, u32[]{:S(2)}, u32[]{:S(2)}) collective-permute-start(f32[8,4,8,128]{3,2,1,0:T(8,128)S(1)} %fusion.7), channel_id=1, source_target_pairs={{0,16},{2,18},{4,20},{6,22},{8,24},{10,26},{12,28},{14,30},{16,0},... | collective-permute-start | bytes 393224 | tf_op jit(solution)/shard_map/ppermute | solution.py:24
  39.9 0.9 broadcast_multiply_fusion
  40.9 0.1 mul.100
  41.0 0.1 fusion.12
  41.1 3.1 %collective-permute-done.5 = f32[8,4,8,128]{3,2,1,0:T(8,128)S(1)} collective-permute-done((f32[8,4,8,128]{3,2,1,0:T(8,128)S(1)}, f32[8,4,8,128]{3,2,1,0:T(8,128)S(1)}, u32[]{:S(2)}, u32[]{:S(2)}) %collective-permute-start.5) | collective-permute-done | bytes 131104 | tf_op jit(solution)/shard_map/ppermute | solution.py:24
  44.3 0.8 multiply_reduce_fusion
  45.1 0.1 reduce_sum.27
  45.2 0.1 reduce_sum.28
  45.4 1.1 %collective-permute-done.6 = f32[2,4]{1,0:T(2,128)S(1)} collective-permute-done((f32[2,4]{1,0:T(2,128)S(1)}, f32[2,4]{1,0:T(2,128)S(1)}, u32[]{:S(2)}, u32[]{:S(2)}) %collective-permute-start.6) | collective-permute-done | bytes 64 | tf_op jit(solution)/shard_map/ppermute | solution.py:24
  46.5 1.7 %collective-permute-start.7 = (f32[2,4]{1,0:T(2,128)S(1)}, f32[2,4]{1,0:T(2,128)S(1)}, u32[]{:S(2)}, u32[]{:S(2)}) collective-permute-start(f32[2,4]{1,0:T(2,128)S(1)} %fusion.14), channel_id=1, source_target_pairs={{0,2},{2,0},{4,6},{6,4},{8,10},{10,8},{12,14},{14,12},{16,18},{18,... | collective-permute-start | bytes 104 | tf_op jit(solution)/shard_map/ppermute | solution.py:24
  48.3 1.9 %collective-permute-done.7 = f32[2,4]{1,0:T(2,128)S(1)} collective-permute-done((f32[2,4]{1,0:T(2,128)S(1)}, f32[2,4]{1,0:T(2,128)S(1)}, u32[]{:S(2)}, u32[]{:S(2)}) %collective-permute-start.7) | collective-permute-done | bytes 64 | tf_op jit(solution)/shard_map/ppermute | solution.py:24
  50.2 0.7 collective-permute-start.8
  50.9 2.9 %collective-permute-done.8 = f32[2,4]{1,0:T(2,128)S(1)} collective-permute-done((f32[2,4]{1,0:T(2,128)S(1)}, f32[2,4]{1,0:T(2,128)S(1)}, u32[]{:S(2)}, u32[]{:S(2)}) %collective-permute-start.8) | collective-permute-done | bytes 64 | tf_op jit(solution)/shard_map/ppermute | solution.py:24
  53.8 3.6 %collective-permute-done.9 = f32[2,4]{1,0:T(2,128)S(1)} collective-permute-done((f32[2,4]{1,0:T(2,128)S(1)}, f32[2,4]{1,0:T(2,128)S(1)}, u32[]{:S(2)}, u32[]{:S(2)}) %collective-permute-start.9) | collective-permute-done | bytes 64 | tf_op jit(solution)/shard_map/ppermute | solution.py:24
  57.4 1.6 %collective-permute-start.10 = (f32[2,4]{1,0:T(2,128)S(1)}, f32[2,4]{1,0:T(2,128)S(1)}, u32[]{:S(2)}, u32[]{:S(2)}) collective-permute-start(f32[2,4]{1,0:T(2,128)S(1)} %add.173), channel_id=1, source_target_pairs={{0,16},{2,18},{4,20},{6,22},{8,24},{10,26},{12,28},{14,30},{16,0},... | collective-permute-start | bytes 104 | tf_op jit(solution)/shard_map/ppermute | solution.py:24
  59.0 2.9 %collective-permute-done.10 = f32[2,4]{1,0:T(2,128)S(1)} collective-permute-done((f32[2,4]{1,0:T(2,128)S(1)}, f32[2,4]{1,0:T(2,128)S(1)}, u32[]{:S(2)}, u32[]{:S(2)}) %collective-permute-start.10) | collective-permute-done | bytes 64 | tf_op jit(solution)/shard_map/ppermute | solution.py:24
  61.9 0.5 fusion.15
  62.5 0.1 mul.105
  62.7 1.7 %collective-permute-start.11 = (f32[8,4,8,128]{3,2,1,0:T(8,128)S(1)}, f32[8,4,8,128]{3,2,1,0:T(8,128)S(1)}, u32[]{:S(2)}, u32[]{:S(2)}) collective-permute-start(f32[8,4,8,128]{3,2,1,0:T(8,128)S(1)} %multiply_subtract_fusion), channel_id=1, source_target_pairs={{0,16},{2,18},{4,20},{6,22},{8,24},{10,26},{12,28},{14,30},{16,0},... | collective-permute-start | bytes 393224 | tf_op jit(solution)/shard_map/ppermute | solution.py:24
  64.4 5.8 %collective-permute-done.11 = f32[8,4,8,128]{3,2,1,0:T(8,128)S(1)} collective-permute-done((f32[8,4,8,128]{3,2,1,0:T(8,128)S(1)}, f32[8,4,8,128]{3,2,1,0:T(8,128)S(1)}, u32[]{:S(2)}, u32[]{:S(2)}) %collective-permute-start.11) | collective-permute-done | bytes 131104 | tf_op jit(solution)/shard_map/ppermute | solution.py:24
  70.2 6.4 %collective-permute-done.12 = f32[8,2,4,8,128]{4,3,2,1,0:T(8,128)S(1)} collective-permute-done((f32[8,2,4,8,128]{4,3,2,1,0:T(8,128)S(1)}, f32[8,2,4,8,128]{4,3,2,1,0:T(8,128)S(1)}, u32[]{:S(2)}, u32[]{:S(2)}) %collective-permute-start.12) | collective-permute-done | bytes 262176 | tf_op jit(solution)/shard_map/ppermute | solution.py:24
  76.7 0.7 collective-permute-start.13
  77.4 1.0 %collective-permute-start.15 = (f32[4,2,2,4,8,128]{5,4,3,2,1,0:T(8,128)S(1)}, f32[4,2,2,4,8,128]{5,4,3,2,1,0:T(8,128)S(1)}, u32[]{:S(2)}, u32[]{:S(2)}) collective-permute-start(f32[4,2,2,4,8,128]{5,4,3,2,1,0:T(8,128)S(1)} %get-tuple-element.19), channel_id=1, source_target_pairs={{0,2},{2,0},{4,6},{6,4},{8,10},{10,8},{12,14},{14,12},{16,18},{18,... | collective-permute-start | bytes 786440 | tf_op jit(solution)/shard_map/ppermute | solution.py:24
  78.5 7.0 %collective-permute-done.13 = f32[4,2,2,4,8,128]{5,4,3,2,1,0:T(8,128)S(1)} collective-permute-done((f32[4,2,2,4,8,128]{5,4,3,2,1,0:T(8,128)S(1)}, f32[4,2,2,4,8,128]{5,4,3,2,1,0:T(8,128)S(1)}, u32[]{:S(2)}, u32[]{:S(2)}) %collective-permute-start.13) | collective-permute-done | bytes 262176 | tf_op jit(solution)/shard_map/ppermute | solution.py:24
  85.5 2.1 %collective-permute-start.14 = (f32[4,2,2,2,4,8,128]{6,5,4,2,1,0,3:T(8,128)S(1)}, f32[4,2,2,2,4,8,128]{6,5,4,2,1,0,3:T(8,128)S(1)}, u32[]{:S(2)}, u32[]{:S(2)}) collective-permute-start(f32[4,2,2,2,4,8,128]{6,5,4,2,1,0,3:T(8,128)S(1)} %pad_maximum_fusion.1), channel_id=1, source_target_pairs={{0,2},{2,0},{4,6},{6,4},{8,10},{10,8},{12,14},{14,12},{16,18},{18,... | collective-permute-start | bytes 1572872 | tf_op jit(solution)/shard_map/ppermute | solution.py:24
  87.7 0.4 collective-permute-start.16
  88.2 6.6 %collective-permute-done.14 = f32[4,2,2,2,4,8,128]{6,5,4,2,1,0,3:T(8,128)S(1)} collective-permute-done((f32[4,2,2,2,4,8,128]{6,5,4,2,1,0,3:T(8,128)S(1)}, f32[4,2,2,2,4,8,128]{6,5,4,2,1,0,3:T(8,128)S(1)}, u32[]{:S(2)}, u32[]{:S(2)}) %collective-permute-start.14) | collective-permute-done | bytes 524320 | tf_op jit(solution)/shard_map/ppermute | solution.py:24
  94.8 0.1 select_bitcast_fusion.3
  94.9 2.1 %collective-permute-done.16 = f32[4,2,2,2,4,8,128]{6,5,4,3,2,1,0:T(8,128)S(1)} collective-permute-done((f32[4,2,2,2,4,8,128]{6,5,4,3,2,1,0:T(8,128)S(1)}, f32[4,2,2,2,4,8,128]{6,5,4,3,2,1,0:T(8,128)S(1)}, u32[]{:S(2)}, u32[]{:S(2)}) %collective-permute-start.16) | collective-permute-done | bytes 524320 | tf_op jit(solution)/shard_map/ppermute | solution.py:24
  97.0 0.1 select_bitcast_fusion.1
  97.1 1.5 %maximum_maximum_fusion = f32[8,2,2,2,2,4,8,128]{7,6,5,4,3,2,1,0:T(8,128)} fusion(f32[4,2,2,1,2,4,8,128]{7,6,5,4,3,2,1,0:T(8,128)S(1)} %get-tuple-element.15, f32[4,2,2,1,2,4,8,128]{7,6,5,4,3,2,1,0:T(8,128)S(1)} %get-tuple-element.14, f32[4,2,2,2,1,4,8,128]{7,6,5,2,1,0,3,4:T(8,128)S(1)} %get-tuple-element.13, ...), kind=kLoop, calls=%fused_computation | loop fusion | flops 1310720 | bytes 4194304 | tf_op jit(solution)/shard_map/concatenate | solution.py:98
  (30 shorter events, 0.8 us)
Async XLA Ops:
  3.2 15.1 %collective-permute-start.2 = (f32[4,2,2,2,4,8,128]{6,5,4,3,2,1,0:T(8,128)}, f32[4,2,2,2,4,8,128]{6,5,4,3,2,1,0:T(8,128)S(1)}, u32[]{:S(2)}, u32[]{:S(2)}) collective-permute-start(f32[4,2,2,2,4,8,128]{6,5,4,3,2,1,0:T(8,128)} %dynamic-slice_bitcast_fusion), channel_id=1, source_target_pairs={{0,4},{2,6},{4,0},{6,2},{8,12},{10,14},{12,8},{14,10},{16,20},{18,... | collective-permute-start | bytes 1572872 | tf_op jit(solution)/shard_map/ppermute | solution.py:24
  7.0 13.9 %collective-permute-start = (f32[4,2,2,2,4,8,128]{6,5,4,3,2,1,0:T(8,128)}, f32[4,2,2,2,4,8,128]{6,5,4,3,2,1,0:T(8,128)S(1)}, u32[]{:S(2)}, u32[]{:S(2)}) collective-permute-start(f32[4,2,2,2,4,8,128]{6,5,4,3,2,1,0:T(8,128)} %dynamic-slice_bitcast_fusion.1), channel_id=1, source_target_pairs={{0,2},{2,0},{4,6},{6,4},{8,10},{10,8},{12,14},{14,12},{16,18},{18,... | collective-permute-start | bytes 1572872 | tf_op jit(solution)/shard_map/ppermute | solution.py:24
  18.4 8.0 %collective-permute-start.3 = (f32[4,2,2,4,8,128]{5,4,3,2,1,0:T(8,128)S(1)}, f32[4,2,2,4,8,128]{5,4,3,2,1,0:T(8,128)}, u32[]{:S(2)}, u32[]{:S(2)}) collective-permute-start(f32[4,2,2,4,8,128]{5,4,3,2,1,0:T(8,128)S(1)} %bitcast_add_fusion), channel_id=1, source_target_pairs={{0,2},{2,0},{4,6},{6,4},{8,10},{10,8},{12,14},{14,12},{16,18},{18,... | collective-permute-start | bytes 786440 | tf_op jit(solution)/shard_map/ppermute | solution.py:24
  21.7 6.9 %collective-permute-start.1 = (f32[4,2,2,4,8,128]{5,4,3,2,1,0:T(8,128)}, f32[4,2,2,4,8,128]{5,4,3,2,1,0:T(8,128)}, u32[]{:S(2)}, u32[]{:S(2)}) collective-permute-start(f32[4,2,2,4,8,128]{5,4,3,2,1,0:T(8,128)} %bitcast_add_fusion.2), channel_id=1, source_target_pairs={{0,4},{2,6},{4,0},{6,2},{8,12},{10,14},{12,8},{14,10},{16,20},{18,... | collective-permute-start | bytes 786440 | tf_op jit(solution)/shard_map/ppermute | solution.py:24
  22.4 18.4 %copy-start.1 = (f32[4]{0:T(128)S(1)}, f32[4]{0:T(128)}, u32[]{:S(2)}) copy-start(f32[4]{0:T(128)} %param.11) | copy-start | bytes 52
  22.4 18.6 %copy-start = (f32[4,16,512]{2,1,0:T(8,128)S(1)}, f32[4,16,512]{2,1,0:T(8,128)}, u32[]{:S(2)}) copy-start(f32[4,16,512]{2,1,0:T(8,128)} %param.7) | copy-start | bytes 393220
  29.6 32.3 %copy-start.2 = (f32[4]{0:T(128)S(1)}, f32[4]{0:T(128)}, u32[]{:S(2)}) copy-start(f32[4]{0:T(128)} %param.10) | copy-start | bytes 52
  29.6 6.4 %collective-permute-start.4 = (f32[8,2,4,8,128]{4,3,2,1,0:T(8,128)S(1)}, f32[8,2,4,8,128]{4,3,2,1,0:T(8,128)S(1)}, u32[]{:S(2)}, u32[]{:S(2)}) collective-permute-start(f32[8,2,4,8,128]{4,3,2,1,0:T(8,128)S(1)} %fusion.2), channel_id=1, source_target_pairs={{0,8},{2,10},{4,12},{6,14},{8,0},{10,2},{12,4},{14,6},{16,24},{18,... | collective-permute-start | bytes 786440 | tf_op jit(solution)/shard_map/ppermute | solution.py:24
  36.1 8.1 %collective-permute-start.5 = (f32[8,4,8,128]{3,2,1,0:T(8,128)S(1)}, f32[8,4,8,128]{3,2,1,0:T(8,128)S(1)}, u32[]{:S(2)}, u32[]{:S(2)}) collective-permute-start(f32[8,4,8,128]{3,2,1,0:T(8,128)S(1)} %fusion.7), channel_id=1, source_target_pairs={{0,16},{2,18},{4,20},{6,22},{8,24},{10,26},{12,28},{14,30},{16,0},... | collective-permute-start | bytes 393224 | tf_op jit(solution)/shard_map/ppermute | solution.py:24
  45.3 1.2 %collective-permute-start.6 = (f32[2,4]{1,0:T(2,128)S(1)}, f32[2,4]{1,0:T(2,128)S(1)}, u32[]{:S(2)}, u32[]{:S(2)}) collective-permute-start(f32[2,4]{1,0:T(2,128)S(1)} %pad_maximum_fusion.5), channel_id=1, source_target_pairs={{0,1},{1,0},{2,3},{3,2},{4,5},{5,4},{6,7},{7,6},{8,9},{9,8},{10,11... | collective-permute-start | bytes 104 | tf_op jit(solution)/shard_map/ppermute | solution.py:24
  46.5 3.6 %collective-permute-start.7 = (f32[2,4]{1,0:T(2,128)S(1)}, f32[2,4]{1,0:T(2,128)S(1)}, u32[]{:S(2)}, u32[]{:S(2)}) collective-permute-start(f32[2,4]{1,0:T(2,128)S(1)} %fusion.14), channel_id=1, source_target_pairs={{0,2},{2,0},{4,6},{6,4},{8,10},{10,8},{12,14},{14,12},{16,18},{18,... | collective-permute-start | bytes 104 | tf_op jit(solution)/shard_map/ppermute | solution.py:24
  50.2 3.6 %collective-permute-start.8 = (f32[2,4]{1,0:T(2,128)S(1)}, f32[2,4]{1,0:T(2,128)S(1)}, u32[]{:S(2)}, u32[]{:S(2)}) collective-permute-start(f32[2,4]{1,0:T(2,128)S(1)} %fusion.18), channel_id=1, source_target_pairs={{0,4},{2,6},{4,0},{6,2},{8,12},{10,14},{12,8},{14,10},{16,20},{18,... | collective-permute-start | bytes 104 | tf_op jit(solution)/shard_map/ppermute | solution.py:24
  53.8 3.6 %collective-permute-start.9 = (f32[2,4]{1,0:T(2,128)S(1)}, f32[2,4]{1,0:T(2,128)S(1)}, u32[]{:S(2)}, u32[]{:S(2)}) collective-permute-start(f32[2,4]{1,0:T(2,128)S(1)} %add.172), channel_id=1, source_target_pairs={{0,8},{2,10},{4,12},{6,14},{8,0},{10,2},{12,4},{14,6},{16,24},{18,... | collective-permute-start | bytes 104 | tf_op jit(solution)/shard_map/ppermute | solution.py:24
  57.4 4.5 %collective-permute-start.10 = (f32[2,4]{1,0:T(2,128)S(1)}, f32[2,4]{1,0:T(2,128)S(1)}, u32[]{:S(2)}, u32[]{:S(2)}) collective-permute-start(f32[2,4]{1,0:T(2,128)S(1)} %add.173), channel_id=1, source_target_pairs={{0,16},{2,18},{4,20},{6,22},{8,24},{10,26},{12,28},{14,30},{16,0},... | collective-permute-start | bytes 104 | tf_op jit(solution)/shard_map/ppermute | solution.py:24
  62.7 7.4 %collective-permute-start.11 = (f32[8,4,8,128]{3,2,1,0:T(8,128)S(1)}, f32[8,4,8,128]{3,2,1,0:T(8,128)S(1)}, u32[]{:S(2)}, u32[]{:S(2)}) collective-permute-start(f32[8,4,8,128]{3,2,1,0:T(8,128)S(1)} %multiply_subtract_fusion), channel_id=1, source_target_pairs={{0,16},{2,18},{4,20},{6,22},{8,24},{10,26},{12,28},{14,30},{16,0},... | collective-permute-start | bytes 393224 | tf_op jit(solution)/shard_map/ppermute | solution.py:24
  70.2 6.4 %collective-permute-start.12 = (f32[8,2,4,8,128]{4,3,2,1,0:T(8,128)S(1)}, f32[8,2,4,8,128]{4,3,2,1,0:T(8,128)S(1)}, u32[]{:S(2)}, u32[]{:S(2)}) collective-permute-start(f32[8,2,4,8,128]{4,3,2,1,0:T(8,128)S(1)} %pad_maximum_fusion.4), channel_id=1, source_target_pairs={{0,8},{2,10},{4,12},{6,14},{8,0},{10,2},{12,4},{14,6},{16,24},{18,... | collective-permute-start | bytes 786440 | tf_op jit(solution)/shard_map/ppermute | solution.py:24
  76.7 8.7 %collective-permute-start.13 = (f32[4,2,2,4,8,128]{5,4,3,2,1,0:T(8,128)S(1)}, f32[4,2,2,4,8,128]{5,4,3,2,1,0:T(8,128)S(1)}, u32[]{:S(2)}, u32[]{:S(2)}) collective-permute-start(f32[4,2,2,4,8,128]{5,4,3,2,1,0:T(8,128)S(1)} %get-tuple-element.18), channel_id=1, source_target_pairs={{0,4},{2,6},{4,0},{6,2},{8,12},{10,14},{12,8},{14,10},{16,20},{18,... | collective-permute-start | bytes 786440 | tf_op jit(solution)/shard_map/ppermute | solution.py:24
  77.4 10.2 %collective-permute-start.15 = (f32[4,2,2,4,8,128]{5,4,3,2,1,0:T(8,128)S(1)}, f32[4,2,2,4,8,128]{5,4,3,2,1,0:T(8,128)S(1)}, u32[]{:S(2)}, u32[]{:S(2)}) collective-permute-start(f32[4,2,2,4,8,128]{5,4,3,2,1,0:T(8,128)S(1)} %get-tuple-element.19), channel_id=1, source_target_pairs={{0,2},{2,0},{4,6},{6,4},{8,10},{10,8},{12,14},{14,12},{16,18},{18,... | collective-permute-start | bytes 786440 | tf_op jit(solution)/shard_map/ppermute | solution.py:24
  85.5 9.2 %collective-permute-start.14 = (f32[4,2,2,2,4,8,128]{6,5,4,2,1,0,3:T(8,128)S(1)}, f32[4,2,2,2,4,8,128]{6,5,4,2,1,0,3:T(8,128)S(1)}, u32[]{:S(2)}, u32[]{:S(2)}) collective-permute-start(f32[4,2,2,2,4,8,128]{6,5,4,2,1,0,3:T(8,128)S(1)} %pad_maximum_fusion.1), channel_id=1, source_target_pairs={{0,2},{2,0},{4,6},{6,4},{8,10},{10,8},{12,14},{14,12},{16,18},{18,... | collective-permute-start | bytes 1572872 | tf_op jit(solution)/shard_map/ppermute | solution.py:24
  87.7 9.2 %collective-permute-start.16 = (f32[4,2,2,2,4,8,128]{6,5,4,3,2,1,0:T(8,128)S(1)}, f32[4,2,2,2,4,8,128]{6,5,4,3,2,1,0:T(8,128)S(1)}, u32[]{:S(2)}, u32[]{:S(2)}) collective-permute-start(f32[4,2,2,2,4,8,128]{6,5,4,3,2,1,0:T(8,128)S(1)} %pad_maximum_fusion.2), channel_id=1, source_target_pairs={{0,4},{2,6},{4,0},{6,2},{8,12},{10,14},{12,8},{14,10},{16,20},{18,... | collective-permute-start | bytes 1572872 | tf_op jit(solution)/shard_map/ppermute | solution.py:24

commit v2 on v1

v2 whole, which is shorter than its diff:
```python
import jax
import jax.numpy as jnp
from jax import lax
from jax.sharding import PartitionSpec as P


STEP = 10
SUB, LANE = 8, 128


def tiles(a):
    t, r, c = a.shape
    a = a.reshape(t, r // SUB, SUB, c // LANE, LANE)
    return a.transpose(0, 1, 3, 2, 4).reshape(t * (r // SUB), c // LANE, SUB, LANE)


def untiles(a, t, r):
    c = a.shape[1]
    a = a.reshape(t, r // SUB, c, SUB, LANE).transpose(0, 1, 3, 2, 4)
    return a.reshape(t, r, c * LANE)


def swap(a, axis, bit):
    n = lax.axis_size(axis)
    return lax.ppermute(a, axis, [(i, i ^ (1 << bit)) for i in range(n)])


class Part:
    def __init__(self, array, low, dims, chosen=()):
        self.array, self.low, self.dims, self.chosen = array, low, dims, dict(chosen)

    def at(self, bit, value):
        return Part(self.array, self.low, self.dims, {**self.chosen, bit: value})

    def read(self, rows):
        block = self.array.shape[1 + len(self.dims) :]
        zero = jnp.uint32(0)
        first = [jnp.uint32(self.low)] + [self.chosen.get(d, zero) for d in self.dims] + [zero] * len(block)
        size = [rows] + [1 if d in self.chosen else 2 for d in self.dims] + list(block)
        left = [2 for d in self.dims if d not in self.chosen]
        return lax.dynamic_slice(self.array, first, size).reshape([rows] + left + list(block))


def total(parts, rows):
    out = parts[0].read(rows)
    for part in parts[1:]:
        out = out + part.read(rows)
    return out


def shards(gradients, weights, first_moment, second_moment, learn_rate, weight_decay):
    n = lax.axis_size("dp")
    bits = n.bit_length() - 1
    me = lax.axis_index("dp")
    b = [((me >> i) & 1).astype(jnp.uint32) for i in range(bits)]
    not_b = [1 - x for x in b]
    g, b, not_b = lax.optimization_barrier((gradients[0], b, not_b))
    nt, rows, _ = weights.shape
    g = tiles(g)
    every = tuple(reversed(range(bits)))
    g = g.reshape((g.shape[0],) + (2,) * bits + (g.shape[1] // n, SUB, LANE))
    half = g.shape[0] // 2
    low = [0, half]
    orders = [(0, 1) + tuple(range(2, bits)), (1, 0) + tuple(range(2, bits))]
    flat = g.reshape(g.shape[: 1 + bits] + (-1, LANE))
    streams = [[Part(g, low[0], every)], [Part(flat, low[1], every)]]
    left = [every, every]
    for phase in range(bits):
        for s in range(2):
            bit = orders[s][phase]
            send = total([p.at(bit, not_b[bit]) for p in streams[s]], half)
            got = swap(send, "dp", bit)
            streams[s] = [p.at(bit, b[bit]) for p in streams[s]]
            left[s] = tuple(d for d in left[s] if d != bit)
            streams[s].append(Part(got, 0, left[s]))
    summed = [(total(p, half) * (1.0 / n)).reshape((half,) + g.shape[-3:]) for p in streams]

    w, m, v = tiles(weights), tiles(first_moment), tiles(second_moment)
    first_fix = 1.0 - 0.9**STEP
    second_fix = 1.0 - 0.999**STEP
    each = nt // 2

    def scaled(factors, s, a):
        factors = factors[s * each : (s + 1) * each]
        return (a.reshape((each, -1) + a.shape[1:]) * factors.reshape((each,) + (1,) * a.ndim)).reshape(a.shape)

    new_first, new_second, update = [], [], []
    for s in range(2):
        own = slice(low[s], low[s] + half)
        first = 0.9 * m[own] + 0.1 * summed[s]
        second = 0.999 * v[own] + 0.001 * summed[s] * summed[s]
        new_first.append(first)
        new_second.append(second)
        step = first / first_fix / (jnp.sqrt(second / second_fix) + 1e-06)
        update.append(step + scaled(weight_decay, s, w[own]))
    new_first, new_second = jnp.concatenate(new_first), jnp.concatenate(new_second)
    update = jnp.concatenate(update)

    def squares(a):
        return jnp.sum((a * a).reshape(nt, -1), axis=1)

    update, sq = lax.optimization_barrier((update, jnp.stack([squares(w), squares(update)])))

    def joined(a, bit, at):
        other = swap(a, "dp", bit)
        low, high = jnp.where(b[bit] == 0, a, other), jnp.where(b[bit] == 0, other, a)
        return jnp.stack([low, high], axis=at)

    def widened(a):
        for bit in reversed(range(2, bits)):
            a = joined(a, bit, 1 + bits - 1 - bit)
        parts = [a[:half], a[half:].reshape((half,) + a.shape[1:-3] + (-1, LANE))]
        return [joined(parts[s], orders[s][1], bits - 1) for s in range(2)]

    wide_w, wide_u = widened(w), widened(update)
    for axis, order in (("mp", range(lax.axis_size("mp").bit_length() - 1)), ("dp", [0, 1] + list(reversed(range(2, bits))))):
        for bit in order:
            sq = sq + swap(sq, axis, bit)
    trust_ratio = jnp.sqrt(sq[0]) / (jnp.sqrt(sq[1]) + 1e-06)
    rate = learn_rate * trust_ratio
    full = [wide_w[s] - scaled(rate, s, wide_u[s]) for s in range(2)]
    full = [joined(full[s], orders[s][0], bits if s == 0 else bits - 1) for s in range(2)]
    full = jnp.concatenate([a.reshape(half, -1, SUB, LANE) for a in full])
    return (
        untiles(full, nt, rows),
        untiles(new_first, nt, rows),
        untiles(new_second, nt, rows),
        trust_ratio,
    )


def solution(mesh):
    in_specs = (
        P("dp", None, "mp", None),
        P(None, "mp", "dp"),
        P(None, "mp", "dp"),
        P(None, "mp", "dp"),
        P(),
        P(),
    )
    out_specs = (P(None, "mp", None), P(None, "mp", "dp"), P(None, "mp", "dp"), P())

    return jax.shard_map(shards, mesh=mesh, in_specs=in_specs, out_specs=out_specs, check_vma=False)
```

time: 98.8 us -> 93.4 us (0.945)
  waiting for transfers between devices: 63 us -> 45.7 us
  starting transfers between devices: 22.5 us -> 32 us
  other arithmetic: 8.41 us -> 9.64 us
  local copies, waits for them, and re-layouts: 3.8 us -> 4.87 us
    ppermute x17 -> x23, waiting for transfers between devices: 63 us -> 45.7 us  [swap(): return lax.ppermute(a, axis, [(i, i ^ 1 << bit) for i in range(n)])]
    ppermute x17 -> x23, starting transfers between devices: 22.5 us -> 32 us  [swap(): return lax.ppermute(a, axis, [(i, i ^ 1 << bit) for i in range(n)])]
    reshape x0 -> x3, local copies, waits for them, and re-layouts: none -> 3.95 us  [the longest x2 3.93 us: read(): lax.dynamic_slice(self.array, first, size)]
    another operation x10 -> x16, other arithmetic: 0.54 us -> 3.7 us  [joined(): return jnp.stack([low, high], axis=at)]
    add x5 -> x8, other arithmetic: 2.8 us -> 0.94 us  [the longest x2 0.76 us: shards(): update.append(step + scaled(weight_decay, s, w[own]))]
    squeeze x2 -> x0, local copies, waits for them, and re-layouts: 1.7 us -> none  [halves(): send.append(lax.dynamic_index_in_dim(a, 1 - b, 1 + at, keepdims=False))]
    slice x1 -> x3, local copies, waits for them, and re-layouts: 1.69 us -> 0.15 us  [the longest x2 0.14 us: scaled(): factors = factors[s * each:(s + 1) * each]]
    concatenate x1 -> x2, other arithmetic: 1.49 us -> 2.19 us  [the longest x1 1.47 us: shards(): full = jnp.concatenate([a.reshape(half, -1, SUB, LANE) for a in full])]
  transfers between devices with their start and end apart: 17 -> 23, of which waited for: 16 -> 20; matrix products, arithmetic and copies ran while one was open for 5% -> 11% of each run, Pallas kernels for 0% -> 0%
where the time goes in v2:
time: 93.4 us; the launch traced here: 93.1 us
  waiting for transfers between devices  45.7 us (49%)
  starting transfers between devices  32 us (34%)
  other arithmetic  9.64 us (10%)
  local copies, waits for them, and re-layouts  4.87 us (5%)
  between operations  0.94 us (1%)
    ppermute x23, waiting for transfers between devices, swap(): return lax.ppermute(a, axis, [(i, i ^ 1 << bit) for i in range(n)])  45.7 us
    ppermute x23, starting transfers between devices, swap(): return lax.ppermute(a, axis, [(i, i ^ 1 << bit) for i in range(n)])  32 us
    reshape x2, local copies, waits for them, and re-layouts, read(): lax.dynamic_slice(self.array, first, size)  3.93 us
    another operation x16, other arithmetic, joined(): return jnp.stack([low, high], axis=at)  3.7 us
  transfers between devices with their start and end apart: 23, of which 20 were waited for; matrix products, arithmetic and copies ran while one was open for 11% of the time, Pallas kernels for 0%

profile of v2, /device:TPU:0, one launch (start us, length us, event | category | flops | bytes accessed | tf_op | source)
XLA Modules:
  0.0 93.1 jit_solution(6815750314240217598)
XLA Ops:
  0.7 2.0 %dynamic-slice_bitcast_fusion.1 = f32[4,2,2,2,4,8,128]{6,5,4,3,2,1,0:T(8,128)} fusion(f32[8,2,2,2,2,4,8,128]{7,6,5,4,3,2,1,0:T(8,128)} %bitcast.213, u32[]{:T(128)S(6)} %sub.18), kind=kLoop, calls=%fused_computation.18 | loop fusion | bytes 1048580 | tf_op jit(solution)/shard_map/reshape | solution.py:41
  2.7 3.0 %collective-permute-start.3 = (f32[4,2,2,2,4,8,128]{6,5,4,3,2,1,0:T(8,128)}, f32[4,2,2,2,4,8,128]{6,5,4,3,2,1,0:T(8,128)S(1)}, u32[]{:S(2)}, u32[]{:S(2)}) collective-permute-start(f32[4,2,2,2,4,8,128]{6,5,4,3,2,1,0:T(8,128)} %dynamic-slice_bitcast_fusion.1), channel_id=1, source_target_pairs={{0,2},{2,0},{4,6},{6,4},{8,10},{10,8},{12,14},{14,12},{16,18},{18,... | collective-permute-start | bytes 1572872 | tf_op jit(solution)/shard_map/ppermute | solution.py:25
  5.7 1.9 %dynamic-slice_bitcast_fusion = f32[4,2,2,2,32,128]{5,4,3,2,1,0:T(8,128)} fusion(f32[8,2,2,2,2,32,128]{6,5,4,3,2,1,0:T(8,128)} %bitcast.214, u32[]{:T(128)S(6)} %sub.19), kind=kLoop, calls=%fused_computation.17 | loop fusion | bytes 1048580 | tf_op jit(solution)/shard_map/reshape | solution.py:41
  7.6 1.5 %collective-permute-start.7 = (f32[4,2,2,2,32,128]{5,4,3,2,1,0:T(8,128)}, f32[4,2,2,2,32,128]{5,4,3,2,1,0:T(8,128)S(1)}, u32[]{:S(2)}, u32[]{:S(2)}) collective-permute-start(f32[4,2,2,2,32,128]{5,4,3,2,1,0:T(8,128)} %dynamic-slice_bitcast_fusion), channel_id=1, source_target_pairs={{0,4},{2,6},{4,0},{6,2},{8,12},{10,14},{12,8},{14,10},{16,20},{18,... | collective-permute-start | bytes 1572872 | tf_op jit(solution)/shard_map/ppermute | solution.py:25
  9.1 2.6 %collective-permute-start = (f32[8,4,8,128]{3,2,1,0:T(8,128)}, f32[8,4,8,128]{3,2,1,0:T(8,128)}, u32[]{:S(2)}, u32[]{:S(2)}) collective-permute-start(f32[8,4,8,128]{3,2,1,0:T(8,128)} %bitcast.224), channel_id=1, source_target_pairs={{0,16},{2,18},{4,20},{6,22},{8,24},{10,26},{12,28},{14,30},{16,0},... | collective-permute-start | bytes 393224 | tf_op jit(solution)/shard_map/ppermute | solution.py:25
  11.7 1.5 %slice_multiply_fusion.2 = (f32[2,2,4,8,128]{4,3,2,1,0:T(8,128)}, f32[2,2,4,8,128]{4,3,2,1,0:T(8,128)}) fusion(f32[4,2,4,8,128]{4,3,2,1,0:T(8,128)} %bitcast.227), kind=kLoop, calls=%fused_computation.58 | loop fusion | flops 32768 | bytes 262144 | tf_op jit(solution)/shard_map/mul | solution.py:91
  13.8 4.0 %collective-permute-done.3 = f32[4,2,2,2,4,8,128]{6,5,4,3,2,1,0:T(8,128)S(1)} collective-permute-done((f32[4,2,2,2,4,8,128]{6,5,4,3,2,1,0:T(8,128)}, f32[4,2,2,2,4,8,128]{6,5,4,3,2,1,0:T(8,128)S(1)}, u32[]{:S(2)}, u32[]{:S(2)}) %collective-permute-start.3) | collective-permute-done | bytes 524320 | tf_op jit(solution)/shard_map/ppermute | solution.py:25
  17.9 1.8 %collective-permute-start.4 = (f32[4,2,2,4,8,128]{5,4,3,2,1,0:T(8,128)S(1)}, f32[4,2,2,4,8,128]{5,4,3,2,1,0:T(8,128)S(1)}, u32[]{:S(2)}, u32[]{:S(2)}) collective-permute-start(f32[4,2,2,4,8,128]{5,4,3,2,1,0:T(8,128)S(1)} %bitcast_add_fusion.1), channel_id=1, source_target_pairs={{0,4},{2,6},{4,0},{6,2},{8,12},{10,14},{12,8},{14,10},{16,20},{18,... | collective-permute-start | bytes 786440 | tf_op jit(solution)/shard_map/ppermute | solution.py:25
  19.7 2.7 %collective-permute-done.7 = f32[4,2,2,2,32,128]{5,4,3,2,1,0:T(8,128)S(1)} collective-permute-done((f32[4,2,2,2,32,128]{5,4,3,2,1,0:T(8,128)}, f32[4,2,2,2,32,128]{5,4,3,2,1,0:T(8,128)S(1)}, u32[]{:S(2)}, u32[]{:S(2)}) %collective-permute-start.7) | collective-permute-done | bytes 524320 | tf_op jit(solution)/shard_map/ppermute | solution.py:25
  22.6 0.9 select_bitcast_fusion.19
  23.5 3.3 %collective-permute-done.4 = f32[4,2,2,4,8,128]{5,4,3,2,1,0:T(8,128)S(1)} collective-permute-done((f32[4,2,2,4,8,128]{5,4,3,2,1,0:T(8,128)S(1)}, f32[4,2,2,4,8,128]{5,4,3,2,1,0:T(8,128)S(1)}, u32[]{:S(2)}, u32[]{:S(2)}) %collective-permute-start.4) | collective-permute-done | bytes 262176 | tf_op jit(solution)/shard_map/ppermute | solution.py:25
  26.8 1.6 %collective-permute-start.5 = (f32[4,2,4,8,128]{4,3,2,1,0:T(8,128)S(1)}, f32[4,2,4,8,128]{4,3,2,1,0:T(8,128)S(1)}, u32[]{:S(2)}, u32[]{:S(2)}) collective-permute-start(f32[4,2,4,8,128]{4,3,2,1,0:T(8,128)S(1)} %bitcast_add_fusion.4), channel_id=1, source_target_pairs={{0,8},{2,10},{4,12},{6,14},{8,0},{10,2},{12,4},{14,6},{16,24},{18,... | collective-permute-start | bytes 393224 | tf_op jit(solution)/shard_map/ppermute | solution.py:25
  28.5 0.5 collective-permute-done.8
  29.0 1.8 %collective-permute-start.9 = (f32[4,2,32,128]{3,2,1,0:T(8,128)S(1)}, f32[4,2,32,128]{3,2,1,0:T(8,128)S(1)}, u32[]{:S(2)}, u32[]{:S(2)}) collective-permute-start(f32[4,2,32,128]{3,2,1,0:T(8,128)S(1)} %bitcast_add_fusion.2), channel_id=1, source_target_pairs={{0,8},{2,10},{4,12},{6,14},{8,0},{10,2},{12,4},{14,6},{16,24},{18,... | collective-permute-start | bytes 393224 | tf_op jit(solution)/shard_map/ppermute | solution.py:25
  30.7 0.7 pad_maximum_fusion.7
  31.8 2.2 %collective-permute-done.5 = f32[4,2,4,8,128]{4,3,2,1,0:T(8,128)S(1)} collective-permute-done((f32[4,2,4,8,128]{4,3,2,1,0:T(8,128)S(1)}, f32[4,2,4,8,128]{4,3,2,1,0:T(8,128)S(1)}, u32[]{:S(2)}, u32[]{:S(2)}) %collective-permute-start.5) | collective-permute-done | bytes 131104 | tf_op jit(solution)/shard_map/ppermute | solution.py:25
  34.0 2.0 %collective-permute-start.6 = (f32[4,4,8,128]{3,2,1,0:T(8,128)S(1)}, f32[4,4,8,128]{3,2,1,0:T(8,128)S(1)}, u32[]{:S(2)}, u32[]{:S(2)}) collective-permute-start(f32[4,4,8,128]{3,2,1,0:T(8,128)S(1)} %bitcast_add_fusion.13), channel_id=1, source_target_pairs={{0,16},{2,18},{4,20},{6,22},{8,24},{10,26},{12,28},{14,30},{16,0},... | collective-permute-start | bytes 196616 | tf_op jit(solution)/shard_map/ppermute | solution.py:25
  35.9 1.5 %collective-permute-done.9 = f32[4,2,32,128]{3,2,1,0:T(8,128)S(1)} collective-permute-done((f32[4,2,32,128]{3,2,1,0:T(8,128)S(1)}, f32[4,2,32,128]{3,2,1,0:T(8,128)S(1)}, u32[]{:S(2)}, u32[]{:S(2)}) %collective-permute-start.9) | collective-permute-done | bytes 131104 | tf_op jit(solution)/shard_map/ppermute | solution.py:25
  37.5 1.7 %collective-permute-start.10 = (f32[4,32,128]{2,1,0:T(8,128)S(1)}, f32[4,32,128]{2,1,0:T(8,128)S(1)}, u32[]{:S(2)}, u32[]{:S(2)}) collective-permute-start(f32[4,32,128]{2,1,0:T(8,128)S(1)} %bitcast_add_fusion.6), channel_id=1, source_target_pairs={{0,16},{2,18},{4,20},{6,22},{8,24},{10,26},{12,28},{14,30},{16,0},... | collective-permute-start | bytes 196616 | tf_op jit(solution)/shard_map/ppermute | solution.py:25
  39.3 1.4 %collective-permute-done.6 = f32[4,4,8,128]{3,2,1,0:T(8,128)S(1)} collective-permute-done((f32[4,4,8,128]{3,2,1,0:T(8,128)S(1)}, f32[4,4,8,128]{3,2,1,0:T(8,128)S(1)}, u32[]{:S(2)}, u32[]{:S(2)}) %collective-permute-start.6) | collective-permute-done | bytes 65568 | tf_op jit(solution)/shard_map/ppermute | solution.py:25
  40.6 0.7 fusion.11
  41.3 1.5 %collective-permute-done.10 = f32[4,32,128]{2,1,0:T(8,128)S(1)} collective-permute-done((f32[4,32,128]{2,1,0:T(8,128)S(1)}, f32[4,32,128]{2,1,0:T(8,128)S(1)}, u32[]{:S(2)}, u32[]{:S(2)}) %collective-permute-start.10) | collective-permute-done | bytes 65568 | tf_op jit(solution)/shard_map/ppermute | solution.py:25
  43.3 2.0 %collective-permute-start.11 = (f32[8,4,8,128]{3,2,1,0:T(8,128)S(1)}, f32[8,4,8,128]{3,2,1,0:T(8,128)S(1)}, u32[]{:S(2)}, u32[]{:S(2)}) collective-permute-start(f32[8,4,8,128]{3,2,1,0:T(8,128)S(1)} %get-tuple-element.24), channel_id=1, source_target_pairs={{0,16},{2,18},{4,20},{6,22},{8,24},{10,26},{12,28},{14,30},{16,0},... | collective-permute-start | bytes 393224 | tf_op jit(solution)/shard_map/ppermute | solution.py:25
  45.2 1.0 %select_bitcast_fusion.15 = (f32[8,2,1,4,8,128]{5,4,3,2,1,0:T(8,128)S(1)}, f32[8,2,1,4,8,128]{5,4,3,2,1,0:T(8,128)S(1)}) fusion(f32[8,2,4,8,128]{4,3,2,1,0:T(8,128)} %collective-permute-done.1, pred[]{:T(512)S(6)} %eq.10, f32[8,1,4,8,128]{4,3,2,1,0:T(8,128)S(1)} %get-tuple-element.55, f32[8,1,4,8,128]{4,3,2,1,0:T(8,128)S(1)} %get-tuple-element.54), kind=kLoop, calls=%fused_computation.40 | loop fusion | flops 196608 | bytes 1048577 | tf_op jit(solution)/shard_map/stack | solution.py:107
  46.3 1.6 %collective-permute-start.2 = (f32[4,2,2,4,8,128]{5,4,3,2,1,0:T(8,128)S(1)}, f32[4,2,2,4,8,128]{5,4,3,2,1,0:T(8,128)S(1)}, u32[]{:S(2)}, u32[]{:S(2)}) collective-permute-start(f32[4,2,2,4,8,128]{5,4,3,2,1,0:T(8,128)S(1)} %get-tuple-element.40), channel_id=1, source_target_pairs={{0,4},{2,6},{4,0},{6,2},{8,12},{10,14},{12,8},{14,10},{16,20},{18,... | collective-permute-start | bytes 786440 | tf_op jit(solution)/shard_map/ppermute | solution.py:25
  47.9 0.4 collective-permute-start.20
  48.3 1.0 %collective-permute-done.11 = f32[8,4,8,128]{3,2,1,0:T(8,128)S(1)} collective-permute-done((f32[8,4,8,128]{3,2,1,0:T(8,128)S(1)}, f32[8,4,8,128]{3,2,1,0:T(8,128)S(1)}, u32[]{:S(2)}, u32[]{:S(2)}) %collective-permute-start.11) | collective-permute-done | bytes 131104 | tf_op jit(solution)/shard_map/ppermute | solution.py:25
  49.3 3.1 %collective-permute-start.12 = (f32[8,2,4,8,128]{4,3,2,1,0:T(8,128)S(1)}, f32[8,2,4,8,128]{4,3,2,1,0:T(8,128)S(1)}, u32[]{:S(2)}, u32[]{:S(2)}) collective-permute-start(f32[8,2,4,8,128]{4,3,2,1,0:T(8,128)S(1)} %pad_maximum_fusion.8), channel_id=1, source_target_pairs={{0,8},{2,10},{4,12},{6,14},{8,0},{10,2},{12,4},{14,6},{16,24},{18,... | collective-permute-start | bytes 786440 | tf_op jit(solution)/shard_map/ppermute | solution.py:25
  52.8 1.5 %collective-permute-done.20 = f32[4,2,2,32,128]{4,3,2,1,0:T(8,128)S(1)} collective-permute-done((f32[4,2,2,32,128]{4,3,2,1,0:T(8,128)S(1)}, f32[4,2,2,32,128]{4,3,2,1,0:T(8,128)S(1)}, u32[]{:S(2)}, u32[]{:S(2)}) %collective-permute-start.20) | collective-permute-done | bytes 262176 | tf_op jit(solution)/shard_map/ppermute | solution.py:25
  54.4 1.1 %collective-permute-done.14 = f32[2,4]{1,0:T(2,128)S(1)} collective-permute-done((f32[2,4]{1,0:T(2,128)S(1)}, f32[2,4]{1,0:T(2,128)S(1)}, u32[]{:S(2)}, u32[]{:S(2)}) %collective-permute-start.14) | collective-permute-done | bytes 64 | tf_op jit(solution)/shard_map/ppermute | solution.py:25
  55.5 0.4 collective-permute-start.15
  55.9 3.2 %collective-permute-done.15 = f32[2,4]{1,0:T(2,128)S(1)} collective-permute-done((f32[2,4]{1,0:T(2,128)S(1)}, f32[2,4]{1,0:T(2,128)S(1)}, u32[]{:S(2)}, u32[]{:S(2)}) %collective-permute-start.15) | collective-permute-done | bytes 64 | tf_op jit(solution)/shard_map/ppermute | solution.py:25
  59.1 0.5 collective-permute-start.16
  59.6 3.1 %collective-permute-done.16 = f32[2,4]{1,0:T(2,128)S(1)} collective-permute-done((f32[2,4]{1,0:T(2,128)S(1)}, f32[2,4]{1,0:T(2,128)S(1)}, u32[]{:S(2)}, u32[]{:S(2)}) %collective-permute-start.16) | collective-permute-done | bytes 64 | tf_op jit(solution)/shard_map/ppermute | solution.py:25
  62.7 0.9 %collective-permute-start.17 = (f32[2,4]{1,0:T(2,128)S(1)}, f32[2,4]{1,0:T(2,128)S(1)}, u32[]{:S(2)}, u32[]{:S(2)}) collective-permute-start(f32[2,4]{1,0:T(2,128)S(1)} %add.133), channel_id=1, source_target_pairs={{0,16},{2,18},{4,20},{6,22},{8,24},{10,26},{12,28},{14,30},{16,0},... | collective-permute-start | bytes 104 | tf_op jit(solution)/shard_map/ppermute | solution.py:25
  63.6 3.5 %collective-permute-done.17 = f32[2,4]{1,0:T(2,128)S(1)} collective-permute-done((f32[2,4]{1,0:T(2,128)S(1)}, f32[2,4]{1,0:T(2,128)S(1)}, u32[]{:S(2)}, u32[]{:S(2)}) %collective-permute-start.17) | collective-permute-done | bytes 64 | tf_op jit(solution)/shard_map/ppermute | solution.py:25
  67.2 2.4 %collective-permute-start.18 = (f32[2,4]{1,0:T(2,128)S(1)}, f32[2,4]{1,0:T(2,128)S(1)}, u32[]{:S(2)}, u32[]{:S(2)}) collective-permute-start(f32[2,4]{1,0:T(2,128)S(1)} %add.134), channel_id=1, source_target_pairs={{0,8},{2,10},{4,12},{6,14},{8,0},{10,2},{12,4},{14,6},{16,24},{18,... | collective-permute-start | bytes 104 | tf_op jit(solution)/shard_map/ppermute | solution.py:25
  69.6 1.6 %collective-permute-done.18 = f32[2,4]{1,0:T(2,128)S(1)} collective-permute-done((f32[2,4]{1,0:T(2,128)S(1)}, f32[2,4]{1,0:T(2,128)S(1)}, u32[]{:S(2)}, u32[]{:S(2)}) %collective-permute-start.18) | collective-permute-done | bytes 64 | tf_op jit(solution)/shard_map/ppermute | solution.py:25
  71.6 0.5 fusion.14
  72.6 1.1 %collective-permute-start.21 = (f32[4,2,2,32,128]{4,3,2,1,0:T(8,128)S(1)}, f32[4,2,2,32,128]{4,3,2,1,0:T(8,128)S(1)}, u32[]{:S(2)}, u32[]{:S(2)}) collective-permute-start(f32[4,2,2,32,128]{4,3,2,1,0:T(8,128)S(1)} %copy.39), channel_id=1, source_target_pairs={{0,2},{2,0},{4,6},{6,4},{8,10},{10,8},{12,14},{14,12},{16,18},{18,... | collective-permute-start | bytes 786440 | tf_op jit(solution)/shard_map/ppermute | solution.py:25
  73.7 4.9 %collective-permute-done.13 = f32[4,2,2,4,8,128]{5,4,3,2,1,0:T(8,128)S(1)} collective-permute-done((f32[4,2,2,4,8,128]{5,4,3,2,1,0:T(8,128)S(1)}, f32[4,2,2,4,8,128]{5,4,3,2,1,0:T(8,128)S(1)}, u32[]{:S(2)}, u32[]{:S(2)}) %collective-permute-start.13) | collective-permute-done | bytes 262176 | tf_op jit(solution)/shard_map/ppermute | solution.py:25
  78.8 1.0 %collective-permute-start.19 = (f32[4,2,2,2,4,8,128]{6,5,4,3,2,1,0:T(8,128)S(1)}, f32[4,2,2,2,4,8,128]{6,5,4,3,2,1,0:T(8,128)S(1)}, u32[]{:S(2)}, u32[]{:S(2)}) collective-permute-start(f32[4,2,2,2,4,8,128]{6,5,4,3,2,1,0:T(8,128)S(1)} %fusion), channel_id=1, source_target_pairs={{0,2},{2,0},{4,6},{6,4},{8,10},{10,8},{12,14},{14,12},{16,18},{18,... | collective-permute-start | bytes 1572872 | tf_op jit(solution)/shard_map/ppermute | solution.py:25
  79.7 2.1 %collective-permute-done.21 = f32[4,2,2,32,128]{4,3,2,1,0:T(8,128)S(1)} collective-permute-done((f32[4,2,2,32,128]{4,3,2,1,0:T(8,128)S(1)}, f32[4,2,2,32,128]{4,3,2,1,0:T(8,128)S(1)}, u32[]{:S(2)}, u32[]{:S(2)}) %collective-permute-start.21) | collective-permute-done | bytes 262176 | tf_op jit(solution)/shard_map/ppermute | solution.py:25
  82.0 1.8 %collective-permute-start.22 = (f32[4,2,2,2,32,128]{5,4,3,2,1,0:T(8,128)S(1)}, f32[4,2,2,2,32,128]{5,4,3,2,1,0:T(8,128)S(1)}, u32[]{:S(2)}, u32[]{:S(2)}) collective-permute-start(f32[4,2,2,2,32,128]{5,4,3,2,1,0:T(8,128)S(1)} %fusion.1), channel_id=1, source_target_pairs={{0,4},{2,6},{4,0},{6,2},{8,12},{10,14},{12,8},{14,10},{16,20},{18,... | collective-permute-start | bytes 1572872 | tf_op jit(solution)/shard_map/ppermute | solution.py:25
  83.8 0.7 pad_maximum_fusion.10
  84.5 5.1 %collective-permute-done.19 = f32[4,2,2,2,4,8,128]{6,5,4,3,2,1,0:T(8,128)S(1)} collective-permute-done((f32[4,2,2,2,4,8,128]{6,5,4,3,2,1,0:T(8,128)S(1)}, f32[4,2,2,2,4,8,128]{6,5,4,3,2,1,0:T(8,128)S(1)}, u32[]{:S(2)}, u32[]{:S(2)}) %collective-permute-start.19) | collective-permute-done | bytes 524320 | tf_op jit(solution)/shard_map/ppermute | solution.py:25
  90.0 1.3 %collective-permute-done.22 = f32[4,2,2,2,32,128]{5,4,3,2,1,0:T(8,128)S(1)} collective-permute-done((f32[4,2,2,2,32,128]{5,4,3,2,1,0:T(8,128)S(1)}, f32[4,2,2,2,32,128]{5,4,3,2,1,0:T(8,128)S(1)}, u32[]{:S(2)}, u32[]{:S(2)}) %collective-permute-start.22) | collective-permute-done | bytes 524320 | tf_op jit(solution)/shard_map/ppermute | solution.py:25
  91.6 1.5 %pad_maximum_fusion = f32[8,64,8,128]{3,2,1,0:T(8,128)} fusion(f32[4,64,8,128]{3,2,1,0:T(8,128)S(1)} %bitcast.212, f32[4,64,8,128]{3,2,1,0:T(8,128)S(1)} %bitcast.211), kind=kLoop, calls=%fused_computation | loop fusion | flops 524288 | bytes 4194304 | tf_op jit(solution)/shard_map/concatenate | solution.py:123
  (70 shorter events, 4.2 us)
Async XLA Ops:
  0.6 17.2 %copy-start = (f32[1,4,16,8192]{3,2,1,0:T(8,128)S(1)}, f32[1,4,16,8192]{3,2,1,0:T(8,128)}, u32[]{:S(2)}) copy-start(f32[1,4,16,8192]{3,2,1,0:T(8,128)} %param.6) | copy-start | bytes 6291460
  0.6 13.0 %copy-start.1 = (f32[4,16,512]{2,1,0:T(8,128)S(1)}, f32[4,16,512]{2,1,0:T(8,128)}, u32[]{:S(2)}) copy-start(f32[4,16,512]{2,1,0:T(8,128)} %param.7) | copy-start | bytes 393220
  0.7 12.6 %copy-start.6 = (f32[4]{0:T(128)S(1)}, f32[4]{0:T(128)}, u32[]{:S(2)}) copy-start(f32[4]{0:T(128)} %param.11) | copy-start | bytes 52
  0.7 13.1 %copy-start.5 = (f32[4,16,512]{2,1,0:T(8,128)S(1)}, f32[4,16,512]{2,1,0:T(8,128)}, u32[]{:S(2)}) copy-start(f32[4,16,512]{2,1,0:T(8,128)} %param.8) | copy-start | bytes 393220
  2.7 15.1 %collective-permute-start.3 = (f32[4,2,2,2,4,8,128]{6,5,4,3,2,1,0:T(8,128)}, f32[4,2,2,2,4,8,128]{6,5,4,3,2,1,0:T(8,128)S(1)}, u32[]{:S(2)}, u32[]{:S(2)}) collective-permute-start(f32[4,2,2,2,4,8,128]{6,5,4,3,2,1,0:T(8,128)} %dynamic-slice_bitcast_fusion.1), channel_id=1, source_target_pairs={{0,2},{2,0},{4,6},{6,4},{8,10},{10,8},{12,14},{14,12},{16,18},{18,... | collective-permute-start | bytes 1572872 | tf_op jit(solution)/shard_map/ppermute | solution.py:25
  7.6 14.9 %collective-permute-start.7 = (f32[4,2,2,2,32,128]{5,4,3,2,1,0:T(8,128)}, f32[4,2,2,2,32,128]{5,4,3,2,1,0:T(8,128)S(1)}, u32[]{:S(2)}, u32[]{:S(2)}) collective-permute-start(f32[4,2,2,2,32,128]{5,4,3,2,1,0:T(8,128)} %dynamic-slice_bitcast_fusion), channel_id=1, source_target_pairs={{0,4},{2,6},{4,0},{6,2},{8,12},{10,14},{12,8},{14,10},{16,20},{18,... | collective-permute-start | bytes 1572872 | tf_op jit(solution)/shard_map/ppermute | solution.py:25
  9.1 13.5 %collective-permute-start = (f32[8,4,8,128]{3,2,1,0:T(8,128)}, f32[8,4,8,128]{3,2,1,0:T(8,128)}, u32[]{:S(2)}, u32[]{:S(2)}) collective-permute-start(f32[8,4,8,128]{3,2,1,0:T(8,128)} %bitcast.224), channel_id=1, source_target_pairs={{0,16},{2,18},{4,20},{6,22},{8,24},{10,26},{12,28},{14,30},{16,0},... | collective-permute-start | bytes 393224 | tf_op jit(solution)/shard_map/ppermute | solution.py:25
  13.8 26.9 %copy-start.3 = (f32[2,2,4,8,128]{4,3,2,1,0:T(8,128)S(1)}, f32[2,2,4,8,128]{4,3,2,1,0:T(8,128)}, u32[]{:S(2)}) copy-start(f32[2,2,4,8,128]{4,3,2,1,0:T(8,128)} %get-tuple-element.60) | copy-start | bytes 196612
  17.9 25.0 %copy-start.2 = (f32[2,2,4,8,128]{4,3,2,1,0:T(8,128)S(1)}, f32[2,2,4,8,128]{4,3,2,1,0:T(8,128)}, u32[]{:S(2)}) copy-start(f32[2,2,4,8,128]{4,3,2,1,0:T(8,128)} %get-tuple-element.61) | copy-start | bytes 196612
  17.9 8.9 %collective-permute-start.4 = (f32[4,2,2,4,8,128]{5,4,3,2,1,0:T(8,128)S(1)}, f32[4,2,2,4,8,128]{5,4,3,2,1,0:T(8,128)S(1)}, u32[]{:S(2)}, u32[]{:S(2)}) collective-permute-start(f32[4,2,2,4,8,128]{5,4,3,2,1,0:T(8,128)S(1)} %bitcast_add_fusion.1), channel_id=1, source_target_pairs={{0,4},{2,6},{4,0},{6,2},{8,12},{10,14},{12,8},{14,10},{16,20},{18,... | collective-permute-start | bytes 786440 | tf_op jit(solution)/shard_map/ppermute | solution.py:25
  22.5 6.4 %collective-permute-start.8 = (f32[4,2,2,32,128]{4,3,2,1,0:T(8,128)S(1)}, f32[4,2,2,32,128]{4,3,2,1,0:T(8,128)S(1)}, u32[]{:S(2)}, u32[]{:S(2)}) collective-permute-start(f32[4,2,2,32,128]{4,3,2,1,0:T(8,128)S(1)} %bitcast_add_fusion), channel_id=1, source_target_pairs={{0,2},{2,0},{4,6},{6,4},{8,10},{10,8},{12,14},{14,12},{16,18},{18,... | collective-permute-start | bytes 786440 | tf_op jit(solution)/shard_map/ppermute | solution.py:25
  26.8 7.1 %collective-permute-start.5 = (f32[4,2,4,8,128]{4,3,2,1,0:T(8,128)S(1)}, f32[4,2,4,8,128]{4,3,2,1,0:T(8,128)S(1)}, u32[]{:S(2)}, u32[]{:S(2)}) collective-permute-start(f32[4,2,4,8,128]{4,3,2,1,0:T(8,128)S(1)} %bitcast_add_fusion.4), channel_id=1, source_target_pairs={{0,8},{2,10},{4,12},{6,14},{8,0},{10,2},{12,4},{14,6},{16,24},{18,... | collective-permute-start | bytes 393224 | tf_op jit(solution)/shard_map/ppermute | solution.py:25
  29.0 8.5 %collective-permute-start.9 = (f32[4,2,32,128]{3,2,1,0:T(8,128)S(1)}, f32[4,2,32,128]{3,2,1,0:T(8,128)S(1)}, u32[]{:S(2)}, u32[]{:S(2)}) collective-permute-start(f32[4,2,32,128]{3,2,1,0:T(8,128)S(1)} %bitcast_add_fusion.2), channel_id=1, source_target_pairs={{0,8},{2,10},{4,12},{6,14},{8,0},{10,2},{12,4},{14,6},{16,24},{18,... | collective-permute-start | bytes 393224 | tf_op jit(solution)/shard_map/ppermute | solution.py:25
  31.5 13.8 %collective-permute-start.1 = (f32[8,2,4,8,128]{4,3,2,1,0:T(8,128)}, f32[8,2,4,8,128]{4,3,2,1,0:T(8,128)}, u32[]{:S(2)}, u32[]{:S(2)}) collective-permute-start(f32[8,2,4,8,128]{4,3,2,1,0:T(8,128)} %pad_maximum_fusion.7), channel_id=1, source_target_pairs={{0,8},{2,10},{4,12},{6,14},{8,0},{10,2},{12,4},{14,6},{16,24},{18,... | collective-permute-start | bytes 786440 | tf_op jit(solution)/shard_map/ppermute | solution.py:25
  34.0 6.6 %collective-permute-start.6 = (f32[4,4,8,128]{3,2,1,0:T(8,128)S(1)}, f32[4,4,8,128]{3,2,1,0:T(8,128)S(1)}, u32[]{:S(2)}, u32[]{:S(2)}) collective-permute-start(f32[4,4,8,128]{3,2,1,0:T(8,128)S(1)} %bitcast_add_fusion.13), channel_id=1, source_target_pairs={{0,16},{2,18},{4,20},{6,22},{8,24},{10,26},{12,28},{14,30},{16,0},... | collective-permute-start | bytes 196616 | tf_op jit(solution)/shard_map/ppermute | solution.py:25
  37.5 5.3 %collective-permute-start.10 = (f32[4,32,128]{2,1,0:T(8,128)S(1)}, f32[4,32,128]{2,1,0:T(8,128)S(1)}, u32[]{:S(2)}, u32[]{:S(2)}) collective-permute-start(f32[4,32,128]{2,1,0:T(8,128)S(1)} %bitcast_add_fusion.6), channel_id=1, source_target_pairs={{0,16},{2,18},{4,20},{6,22},{8,24},{10,26},{12,28},{14,30},{16,0},... | collective-permute-start | bytes 196616 | tf_op jit(solution)/shard_map/ppermute | solution.py:25
  43.3 6.0 %collective-permute-start.11 = (f32[8,4,8,128]{3,2,1,0:T(8,128)S(1)}, f32[8,4,8,128]{3,2,1,0:T(8,128)S(1)}, u32[]{:S(2)}, u32[]{:S(2)}) collective-permute-start(f32[8,4,8,128]{3,2,1,0:T(8,128)S(1)} %get-tuple-element.24), channel_id=1, source_target_pairs={{0,16},{2,18},{4,20},{6,22},{8,24},{10,26},{12,28},{14,30},{16,0},... | collective-permute-start | bytes 393224 | tf_op jit(solution)/shard_map/ppermute | solution.py:25
  46.3 6.4 %collective-permute-start.2 = (f32[4,2,2,4,8,128]{5,4,3,2,1,0:T(8,128)S(1)}, f32[4,2,2,4,8,128]{5,4,3,2,1,0:T(8,128)S(1)}, u32[]{:S(2)}, u32[]{:S(2)}) collective-permute-start(f32[4,2,2,4,8,128]{5,4,3,2,1,0:T(8,128)S(1)} %get-tuple-element.40), channel_id=1, source_target_pairs={{0,4},{2,6},{4,0},{6,2},{8,12},{10,14},{12,8},{14,10},{16,20},{18,... | collective-permute-start | bytes 786440 | tf_op jit(solution)/shard_map/ppermute | solution.py:25
  47.9 6.4 %collective-permute-start.20 = (f32[4,2,2,32,128]{4,3,2,1,0:T(8,128)S(1)}, f32[4,2,2,32,128]{4,3,2,1,0:T(8,128)S(1)}, u32[]{:S(2)}, u32[]{:S(2)}) collective-permute-start(f32[4,2,2,32,128]{4,3,2,1,0:T(8,128)S(1)} %get-tuple-element.41), channel_id=1, source_target_pairs={{0,2},{2,0},{4,6},{6,4},{8,10},{10,8},{12,14},{14,12},{16,18},{18,... | collective-permute-start | bytes 786440 | tf_op jit(solution)/shard_map/ppermute | solution.py:25
  49.3 21.8 %collective-permute-start.12 = (f32[8,2,4,8,128]{4,3,2,1,0:T(8,128)S(1)}, f32[8,2,4,8,128]{4,3,2,1,0:T(8,128)S(1)}, u32[]{:S(2)}, u32[]{:S(2)}) collective-permute-start(f32[8,2,4,8,128]{4,3,2,1,0:T(8,128)S(1)} %pad_maximum_fusion.8), channel_id=1, source_target_pairs={{0,8},{2,10},{4,12},{6,14},{8,0},{10,2},{12,4},{14,6},{16,24},{18,... | collective-permute-start | bytes 786440 | tf_op jit(solution)/shard_map/ppermute | solution.py:25
  52.8 18.8 %copy-start.7 = (f32[4]{0:T(128)S(1)}, f32[4]{0:T(128)}, u32[]{:S(2)}) copy-start(f32[4]{0:T(128)} %param.10) | copy-start | bytes 52
  54.3 1.2 %collective-permute-start.14 = (f32[2,4]{1,0:T(2,128)S(1)}, f32[2,4]{1,0:T(2,128)S(1)}, u32[]{:S(2)}, u32[]{:S(2)}) collective-permute-start(f32[2,4]{1,0:T(2,128)S(1)} %pad_maximum_fusion.12), channel_id=1, source_target_pairs={{0,1},{1,0},{2,3},{3,2},{4,5},{5,4},{6,7},{7,6},{8,9},{9,8},{10,11... | collective-permute-start | bytes 104 | tf_op jit(solution)/shard_map/ppermute | solution.py:25
  55.5 3.6 %collective-permute-start.15 = (f32[2,4]{1,0:T(2,128)S(1)}, f32[2,4]{1,0:T(2,128)S(1)}, u32[]{:S(2)}, u32[]{:S(2)}) collective-permute-start(f32[2,4]{1,0:T(2,128)S(1)} %add.131), channel_id=1, source_target_pairs={{0,2},{2,0},{4,6},{6,4},{8,10},{10,8},{12,14},{14,12},{16,18},{18,... | collective-permute-start | bytes 104 | tf_op jit(solution)/shard_map/ppermute | solution.py:25
  59.1 3.6 %collective-permute-start.16 = (f32[2,4]{1,0:T(2,128)S(1)}, f32[2,4]{1,0:T(2,128)S(1)}, u32[]{:S(2)}, u32[]{:S(2)}) collective-permute-start(f32[2,4]{1,0:T(2,128)S(1)} %add.132), channel_id=1, source_target_pairs={{0,4},{2,6},{4,0},{6,2},{8,12},{10,14},{12,8},{14,10},{16,20},{18,... | collective-permute-start | bytes 104 | tf_op jit(solution)/shard_map/ppermute | solution.py:25
  62.7 4.5 %collective-permute-start.17 = (f32[2,4]{1,0:T(2,128)S(1)}, f32[2,4]{1,0:T(2,128)S(1)}, u32[]{:S(2)}, u32[]{:S(2)}) collective-permute-start(f32[2,4]{1,0:T(2,128)S(1)} %add.133), channel_id=1, source_target_pairs={{0,16},{2,18},{4,20},{6,22},{8,24},{10,26},{12,28},{14,30},{16,0},... | collective-permute-start | bytes 104 | tf_op jit(solution)/shard_map/ppermute | solution.py:25
  67.2 3.9 %collective-permute-start.18 = (f32[2,4]{1,0:T(2,128)S(1)}, f32[2,4]{1,0:T(2,128)S(1)}, u32[]{:S(2)}, u32[]{:S(2)}) collective-permute-start(f32[2,4]{1,0:T(2,128)S(1)} %add.134), channel_id=1, source_target_pairs={{0,8},{2,10},{4,12},{6,14},{8,0},{10,2},{12,4},{14,6},{16,24},{18,... | collective-permute-start | bytes 104 | tf_op jit(solution)/shard_map/ppermute | solution.py:25
  71.3 7.3 %collective-permute-start.13 = (f32[4,2,2,4,8,128]{5,4,3,2,1,0:T(8,128)S(1)}, f32[4,2,2,4,8,128]{5,4,3,2,1,0:T(8,128)S(1)}, u32[]{:S(2)}, u32[]{:S(2)}) collective-permute-start(f32[4,2,2,4,8,128]{5,4,3,2,1,0:T(8,128)S(1)} %copy.44), channel_id=1, source_target_pairs={{0,4},{2,6},{4,0},{6,2},{8,12},{10,14},{12,8},{14,10},{16,20},{18,... | collective-permute-start | bytes 786440 | tf_op jit(solution)/shard_map/ppermute | solution.py:25
  72.6 9.2 %collective-permute-start.21 = (f32[4,2,2,32,128]{4,3,2,1,0:T(8,128)S(1)}, f32[4,2,2,32,128]{4,3,2,1,0:T(8,128)S(1)}, u32[]{:S(2)}, u32[]{:S(2)}) collective-permute-start(f32[4,2,2,32,128]{4,3,2,1,0:T(8,128)S(1)} %copy.39), channel_id=1, source_target_pairs={{0,2},{2,0},{4,6},{6,4},{8,10},{10,8},{12,14},{14,12},{16,18},{18,... | collective-permute-start | bytes 786440 | tf_op jit(solution)/shard_map/ppermute | solution.py:25
  78.6 5.2 %copy-start.4 = (f32[4,4,8,128]{3,2,1,0:T(8,128)S(1)}, f32[4,4,8,128]{3,2,1,0:T(8,128)}, u32[]{:S(2)}) copy-start(f32[4,4,8,128]{3,2,1,0:T(8,128)} %get-tuple-element.30) | copy-start | bytes 196612
  78.8 10.9 %collective-permute-start.19 = (f32[4,2,2,2,4,8,128]{6,5,4,3,2,1,0:T(8,128)S(1)}, f32[4,2,2,2,4,8,128]{6,5,4,3,2,1,0:T(8,128)S(1)}, u32[]{:S(2)}, u32[]{:S(2)}) collective-permute-start(f32[4,2,2,2,4,8,128]{6,5,4,3,2,1,0:T(8,128)S(1)} %fusion), channel_id=1, source_target_pairs={{0,2},{2,0},{4,6},{6,4},{8,10},{10,8},{12,14},{14,12},{16,18},{18,... | collective-permute-start | bytes 1572872 | tf_op jit(solution)/shard_map/ppermute | solution.py:25
  82.0 9.2 %collective-permute-start.22 = (f32[4,2,2,2,32,128]{5,4,3,2,1,0:T(8,128)S(1)}, f32[4,2,2,2,32,128]{5,4,3,2,1,0:T(8,128)S(1)}, u32[]{:S(2)}, u32[]{:S(2)}) collective-permute-start(f32[4,2,2,2,32,128]{5,4,3,2,1,0:T(8,128)S(1)} %fusion.1), channel_id=1, source_target_pairs={{0,4},{2,6},{4,0},{6,2},{8,12},{10,14},{12,8},{14,10},{16,20},{18,... | collective-permute-start | bytes 1572872 | tf_op jit(solution)/shard_map/ppermute | solution.py:25
